TPU v7x, 32 devices: a whole 2x2x4 slice. The times are simulated.
32 devices in a mesh: mode: 8 (over y, x, core), rows: 4 (over z).
Axes of the slice: x: 2, y: 2, z: 4, core: 2. Of those that a mesh axis runs over, the one named last changes fastest.
Arguments:
- tangents: float32 [128, 3, 32, 1024], P('mode', None, 'rows'), may hold values from -6 to 6
- checkpoints: float32 [8, 3, 32, 1024], P(None, None, 'rows', 'mode'), may hold values from 0 to 0.5
- owner_order: int32 [8], replicated, may hold values from 0 to 7, each once
- land_mask: int32 [32, 1024], P('rows'), may hold values 0 or 1
- coefficients: float32 [128, 128], replicated, may hold values from -0.9 to 0.9
Outputs:
- vectors: float32 [128, 3, 32, 1024], P(None, None, 'rows', 'mode')
Inputs may be any that keep to these rules, and one draw needn't show every extreme that they name: `owner_order`: every checkpoint slot is named by exactly one step.
All inputs are finite; a program needn't handle non-finite values. No bound on the sum of `land_mask` on one device may be relied on, other than what follows from the above.
Results may differ from a plain program's by a relative error of at most 0.0002.
Values sent between devices are 32-bit elements; how exact they have to be, the bound alone decides.
A program may use at most 64 MiB of HBM per device.

v0:
```python
import jax
import jax.numpy as jnp
from jax import lax
from jax.sharding import PartitionSpec as P

mean_depth = 1.0
gravity = 1.0
coriolis = 0.5
time_step = 0.5


def padded(cells, sides, width):
    for axis, dim in sides:
        count = lax.axis_size(axis)
        ends = count - 1
        head = lax.slice_in_dim(cells, 0, width, axis=dim)
        tail = lax.slice_in_dim(cells, cells.shape[dim] - width, cells.shape[dim], axis=dim)
        cells = jnp.concatenate(
            [
                lax.ppermute(tail, axis, [(i, (i + 1) % count) for i in range(ends)]),
                cells,
                lax.ppermute(head, axis, [((i + 1) % count, i) for i in range(ends)]),
            ],
            axis=dim,
        )
    return cells


def deriv_x(values):
    return 0.5 * (jnp.roll(values, -1, -1) - jnp.roll(values, 1, -1))


def deriv_y(values):
    return 0.5 * (values[..., 2:, :] - values[..., :-2, :])


def interior(values):
    return values[..., 1:-1, :]


def tendency(base_flow, current):
    depth_total = mean_depth + base_flow[0]
    flow_u = base_flow[1]
    flow_v = base_flow[2]
    height = current[:, 0]
    zonal = current[:, 1]
    meridional = current[:, 2]
    flux_x = depth_total * zonal + height * flow_u
    flux_y = depth_total * meridional + height * flow_v
    height_rate = -(interior(deriv_x(flux_x)) + deriv_y(flux_y))
    zonal_mid = interior(zonal)
    merid_mid = interior(meridional)
    flow_umid = interior(flow_u)
    flow_vmid = interior(flow_v)
    zonal_rate = (
        -(
            flow_umid * interior(deriv_x(zonal))
            + zonal_mid * interior(deriv_x(flow_u))
            + flow_vmid * deriv_y(zonal)
            + merid_mid * deriv_y(flow_u)
        )
        + coriolis * merid_mid
        - gravity * interior(deriv_x(height))
    )
    merid_rate = (
        -(
            flow_umid * interior(deriv_x(meridional))
            + zonal_mid * interior(deriv_x(flow_v))
            + flow_vmid * deriv_y(meridional)
            + merid_mid * deriv_y(flow_v)
        )
        - coriolis * zonal_mid
        - gravity * deriv_y(height)
    )
    return jnp.stack([height_rate, zonal_rate, merid_rate], 1)


def step_wide(base_wide, state_wide, wet_wide):
    slope_one = tendency(base_wide, state_wide)
    middle = wet_wide[1:-1] * (state_wide[:, :, 1:-1] + time_step * slope_one)
    slope_two = tendency(base_wide[:, 1:-1], middle)
    return wet_wide[2:-2] * (
        state_wide[:, :, 2:-2] + 0.5 * time_step * (slope_one[:, :, 1:-1] + slope_two)
    )


def on_device(tangents, checkpoints, owner_order, land_mask, coefficients):
    wet_mask = land_mask.astype(jnp.float32)
    current = wet_mask * tangents
    depth = 2
    flows_wide, wet_stack = (
        padded(checkpoints, (("rows", 2),), depth),
        padded(wet_mask[None, None], (("rows", 2),), depth),
    )
    wet_wide = wet_stack[0, 0]

    def fetch_flow(step_index):
        held_tile = lax.dynamic_index_in_dim(flows_wide, owner_order[step_index], 0, keepdims=False)
        return lax.all_gather(held_tile, "mode", axis=2, tiled=True)

    total_steps = owner_order.shape[0]

    def advance(step_index, current):
        widened = padded(current, (("rows", 2),), 2)
        return step_wide(fetch_flow(step_index), widened, wet_wide)

    final = lax.fori_loop(0, total_steps, advance, current)
    mixing = jnp.eye(coefficients.shape[0], dtype=jnp.float32) + jnp.triu(coefficients)
    cell_block = lax.all_to_all(final, "mode", split_axis=3, concat_axis=0, tiled=True)
    flattened = cell_block.reshape(cell_block.shape[0], -1)
    mixed = jnp.dot(
        mixing.T, flattened, precision=lax.Precision.HIGHEST, preferred_element_type=jnp.float32
    )
    return mixed.reshape(cell_block.shape)


def solution(mesh):
    placed = (
        P("mode", None, "rows", None),
        P(None, None, "rows", "mode"),
        P(),
        P("rows", None),
        P(),
    )
    return jax.shard_map(
        on_device,
        mesh=mesh,
        in_specs=placed,
        out_specs=P(None, None, "rows", "mode"),
        check_vma=False,
    )
```

profile of v0, /device:TPU:0, one launch (start us, length us, event | category | flops | bytes accessed | tf_op | source)
XLA Modules:
  0.0 402.4 jit_solution(8135360196230346554)
XLA Ops:
  1.0 5.0 %collective-permute-start.4 = (f32[8,3,2,128]{3,2,1,0:T(2,128)S(1)}, f32[8,3,2,128]{3,2,1,0:T(2,128)S(1)}, u32[]{:S(2)}, u32[]{:S(2)}) collective-permute-start(f32[8,3,2,128]{3,2,1,0:T(2,128)S(1)} %get-tuple-element.196), channel_id=1, source_target_pairs={{0,1},{1,2},{2,3},{4,5},{5,6},{6,7},{8,9},{9,10},{10,11},{12,13},{... | collective-permute-start | bytes 73736 | tf_op jit(solution)/shard_map/ppermute | solution.py:20
  8.0 4.5 %collective-permute-start.2 = (f32[1,1,2,1024]{3,2,1,0:T(2,128)S(1)}, f32[1,1,2,1024]{3,2,1,0:T(2,128)S(1)}, u32[]{:S(2)}, u32[]{:S(2)}) collective-permute-start(f32[1,1,2,1024]{3,2,1,0:T(2,128)S(1)} %get-tuple-element.198), channel_id=1, source_target_pairs={{0,1},{1,2},{2,3},{4,5},{5,6},{6,7},{8,9},{9,10},{10,11},{12,13},{... | collective-permute-start | bytes 24584 | tf_op jit(solution)/shard_map/ppermute | solution.py:20
  18.8 316.0 %while.13 = (s32[]{:T(128)}, f32[16,3,8,1024]{3,2,1,0:T(8,128)S(1)}, f32[12,1024]{1,0:T(8,128)}, s32[8]{0:T(128)S(1)}, f32[8,3,12,128]{3,2,1,0:T(8,128)S(1)}, /*...) while((s32[]{:T(128)}, f32[16,3,8,1024]{3,2,1,0:T(8,128)S(1)}, f32[12,1024]{1,0:T(8,128)}, s32[8]{0:T(128)S(1)}, ...), condition=%wide.region_1.2_spmd, body=%wide.region_0.1_spmd.sunk | while | flops 21987332 | bytes 97589864 | solution.py:107
  20.5 5.3 %collective-permute-start.1 = (f32[16,3,2,1024]{3,2,0,1:T(2,128)S(1)}, f32[16,3,2,1024]{3,2,0,1:T(2,128)}, u32[]{:S(2)}, u32[]{:S(2)}) collective-permute-start(f32[16,3,2,1024]{3,2,0,1:T(2,128)S(1)} %get-tuple-element.308), channel_id=1, source_target_pairs={{0,1},{1,2},{2,3},{4,5},{5,6},{6,7},{8,9},{9,10},{10,11},{12,13},{... | collective-permute-start | bytes 1179656 | tf_op jit(solution)/shard_map/while/body/eval_jaxpr/ppermute | solution.py:20
  28.5 9.6 %all-gather.2 = f32[1,3,12,1024]{3,2,1,0:T(8,128)S(1)} all-gather(f32[1,3,12,128]{3,2,1,0:T(8,128)S(1)} %constant_dynamic-slice_fusion.2), channel_id=2, replica_groups=mesh['mode'=8,'rows'=4] {'mode'}, dimensions={3}, use_global_device_ids=true | all-gather | bytes 165888 | tf_op jit(solution)/shard_map/while/body/eval_jaxpr/all_gather | solution.py:99
  60.3 5.3 %collective-permute-start.1 = (f32[16,3,2,1024]{3,2,0,1:T(2,128)S(1)}, f32[16,3,2,1024]{3,2,0,1:T(2,128)}, u32[]{:S(2)}, u32[]{:S(2)}) collective-permute-start(f32[16,3,2,1024]{3,2,0,1:T(2,128)S(1)} %get-tuple-element.308), channel_id=1, source_target_pairs={{0,1},{1,2},{2,3},{4,5},{5,6},{6,7},{8,9},{9,10},{10,11},{12,13},{... | collective-permute-start | bytes 1179656 | tf_op jit(solution)/shard_map/while/body/eval_jaxpr/ppermute | solution.py:20
  68.4 9.6 %all-gather.2 = f32[1,3,12,1024]{3,2,1,0:T(8,128)S(1)} all-gather(f32[1,3,12,128]{3,2,1,0:T(8,128)S(1)} %constant_dynamic-slice_fusion.2), channel_id=2, replica_groups=mesh['mode'=8,'rows'=4] {'mode'}, dimensions={3}, use_global_device_ids=true | all-gather | bytes 165888 | tf_op jit(solution)/shard_map/while/body/eval_jaxpr/all_gather | solution.py:99
  100.2 5.3 %collective-permute-start.1 = (f32[16,3,2,1024]{3,2,0,1:T(2,128)S(1)}, f32[16,3,2,1024]{3,2,0,1:T(2,128)}, u32[]{:S(2)}, u32[]{:S(2)}) collective-permute-start(f32[16,3,2,1024]{3,2,0,1:T(2,128)S(1)} %get-tuple-element.308), channel_id=1, source_target_pairs={{0,1},{1,2},{2,3},{4,5},{5,6},{6,7},{8,9},{9,10},{10,11},{12,13},{... | collective-permute-start | bytes 1179656 | tf_op jit(solution)/shard_map/while/body/eval_jaxpr/ppermute | solution.py:20
  108.2 8.6 %all-gather.2 = f32[1,3,12,1024]{3,2,1,0:T(8,128)S(1)} all-gather(f32[1,3,12,128]{3,2,1,0:T(8,128)S(1)} %constant_dynamic-slice_fusion.2), channel_id=2, replica_groups=mesh['mode'=8,'rows'=4] {'mode'}, dimensions={3}, use_global_device_ids=true | all-gather | bytes 165888 | tf_op jit(solution)/shard_map/while/body/eval_jaxpr/all_gather | solution.py:99
  139.0 5.3 %collective-permute-start.1 = (f32[16,3,2,1024]{3,2,0,1:T(2,128)S(1)}, f32[16,3,2,1024]{3,2,0,1:T(2,128)}, u32[]{:S(2)}, u32[]{:S(2)}) collective-permute-start(f32[16,3,2,1024]{3,2,0,1:T(2,128)S(1)} %get-tuple-element.308), channel_id=1, source_target_pairs={{0,1},{1,2},{2,3},{4,5},{5,6},{6,7},{8,9},{9,10},{10,11},{12,13},{... | collective-permute-start | bytes 1179656 | tf_op jit(solution)/shard_map/while/body/eval_jaxpr/ppermute | solution.py:20
  147.1 9.6 %all-gather.2 = f32[1,3,12,1024]{3,2,1,0:T(8,128)S(1)} all-gather(f32[1,3,12,128]{3,2,1,0:T(8,128)S(1)} %constant_dynamic-slice_fusion.2), channel_id=2, replica_groups=mesh['mode'=8,'rows'=4] {'mode'}, dimensions={3}, use_global_device_ids=true | all-gather | bytes 165888 | tf_op jit(solution)/shard_map/while/body/eval_jaxpr/all_gather | solution.py:99
  178.9 5.3 %collective-permute-start.1 = (f32[16,3,2,1024]{3,2,0,1:T(2,128)S(1)}, f32[16,3,2,1024]{3,2,0,1:T(2,128)}, u32[]{:S(2)}, u32[]{:S(2)}) collective-permute-start(f32[16,3,2,1024]{3,2,0,1:T(2,128)S(1)} %get-tuple-element.308), channel_id=1, source_target_pairs={{0,1},{1,2},{2,3},{4,5},{5,6},{6,7},{8,9},{9,10},{10,11},{12,13},{... | collective-permute-start | bytes 1179656 | tf_op jit(solution)/shard_map/while/body/eval_jaxpr/ppermute | solution.py:20
  186.9 8.6 %all-gather.2 = f32[1,3,12,1024]{3,2,1,0:T(8,128)S(1)} all-gather(f32[1,3,12,128]{3,2,1,0:T(8,128)S(1)} %constant_dynamic-slice_fusion.2), channel_id=2, replica_groups=mesh['mode'=8,'rows'=4] {'mode'}, dimensions={3}, use_global_device_ids=true | all-gather | bytes 165888 | tf_op jit(solution)/shard_map/while/body/eval_jaxpr/all_gather | solution.py:99
  217.8 5.3 %collective-permute-start.1 = (f32[16,3,2,1024]{3,2,0,1:T(2,128)S(1)}, f32[16,3,2,1024]{3,2,0,1:T(2,128)}, u32[]{:S(2)}, u32[]{:S(2)}) collective-permute-start(f32[16,3,2,1024]{3,2,0,1:T(2,128)S(1)} %get-tuple-element.308), channel_id=1, source_target_pairs={{0,1},{1,2},{2,3},{4,5},{5,6},{6,7},{8,9},{9,10},{10,11},{12,13},{... | collective-permute-start | bytes 1179656 | tf_op jit(solution)/shard_map/while/body/eval_jaxpr/ppermute | solution.py:20
  225.8 9.6 %all-gather.2 = f32[1,3,12,1024]{3,2,1,0:T(8,128)S(1)} all-gather(f32[1,3,12,128]{3,2,1,0:T(8,128)S(1)} %constant_dynamic-slice_fusion.2), channel_id=2, replica_groups=mesh['mode'=8,'rows'=4] {'mode'}, dimensions={3}, use_global_device_ids=true | all-gather | bytes 165888 | tf_op jit(solution)/shard_map/while/body/eval_jaxpr/all_gather | solution.py:99
  257.6 5.3 %collective-permute-start.1 = (f32[16,3,2,1024]{3,2,0,1:T(2,128)S(1)}, f32[16,3,2,1024]{3,2,0,1:T(2,128)}, u32[]{:S(2)}, u32[]{:S(2)}) collective-permute-start(f32[16,3,2,1024]{3,2,0,1:T(2,128)S(1)} %get-tuple-element.308), channel_id=1, source_target_pairs={{0,1},{1,2},{2,3},{4,5},{5,6},{6,7},{8,9},{9,10},{10,11},{12,13},{... | collective-permute-start | bytes 1179656 | tf_op jit(solution)/shard_map/while/body/eval_jaxpr/ppermute | solution.py:20
  265.6 8.6 %all-gather.2 = f32[1,3,12,1024]{3,2,1,0:T(8,128)S(1)} all-gather(f32[1,3,12,128]{3,2,1,0:T(8,128)S(1)} %constant_dynamic-slice_fusion.2), channel_id=2, replica_groups=mesh['mode'=8,'rows'=4] {'mode'}, dimensions={3}, use_global_device_ids=true | all-gather | bytes 165888 | tf_op jit(solution)/shard_map/while/body/eval_jaxpr/all_gather | solution.py:99
  296.5 5.3 %collective-permute-start.1 = (f32[16,3,2,1024]{3,2,0,1:T(2,128)S(1)}, f32[16,3,2,1024]{3,2,0,1:T(2,128)}, u32[]{:S(2)}, u32[]{:S(2)}) collective-permute-start(f32[16,3,2,1024]{3,2,0,1:T(2,128)S(1)} %get-tuple-element.308), channel_id=1, source_target_pairs={{0,1},{1,2},{2,3},{4,5},{5,6},{6,7},{8,9},{9,10},{10,11},{12,13},{... | collective-permute-start | bytes 1179656 | tf_op jit(solution)/shard_map/while/body/eval_jaxpr/ppermute | solution.py:20
  304.5 9.6 %all-gather.2 = f32[1,3,12,1024]{3,2,1,0:T(8,128)S(1)} all-gather(f32[1,3,12,128]{3,2,1,0:T(8,128)S(1)} %constant_dynamic-slice_fusion.2), channel_id=2, replica_groups=mesh['mode'=8,'rows'=4] {'mode'}, dimensions={3}, use_global_device_ids=true | all-gather | bytes 165888 | tf_op jit(solution)/shard_map/while/body/eval_jaxpr/all_gather | solution.py:99
  334.9 7.4 %copy.42 = f32[16,3,8,1024]{0,2,1,3:T(8,128)} copy(f32[16,3,8,1024]{3,2,1,0:T(8,128)S(1)} %get-tuple-element.418) | data formatting | bytes 3145728 | tf_op jit(solution)/shard_map/while | solution.py:107
  342.3 9.8 %reshape.42 = f32[8,1,49152]{2,1,0:T(1,128)} reshape(f32[1024,3,8,16]{3,2,1,0:T(8,128)} %bitcast.127) | data formatting | bytes 3145728
  355.7 20.9 %all-to-all-done = f32[8,1,49152]{2,1,0:T(1,128)S(1)} async-done(((f32[8,1,49152]{2,1,0:T(1,128)}), f32[8,1,49152]{2,1,0:T(1,128)S(1)}, u32[]{:S(2)}, u32[]{:S(2)}) %all-to-all-start) | async-done | bytes 1572896 | tf_op jit(solution)/shard_map/all_to_all | solution.py:109
  381.5 8.7 %reshape.43 = f32[1024,3,8,16]{3,2,1,0:T(8,128)} reshape(f32[8,49152]{1,0:T(8,128)S(1)} %reduce) | data formatting | bytes 3145728
  390.2 7.5 %copy.43 = f32[16,3,8,8,128]{4,2,1,0,3:T(8,128)S(1)} copy(f32[16,3,8,8,128]{0,2,1,4,3:T(8,128)} %bitcast.128) | data formatting | bytes 3145728 | tf_op jit(solution)/shard_map/all_to_all | solution.py:109
  (546 shorter events, 203.2 us)
Async XLA Ops:
  1.0 17.8 %collective-permute-start.4 = (f32[8,3,2,128]{3,2,1,0:T(2,128)S(1)}, f32[8,3,2,128]{3,2,1,0:T(2,128)S(1)}, u32[]{:S(2)}, u32[]{:S(2)}) collective-permute-start(f32[8,3,2,128]{3,2,1,0:T(2,128)S(1)} %get-tuple-element.196), channel_id=1, source_target_pairs={{0,1},{1,2},{2,3},{4,5},{5,6},{6,7},{8,9},{9,10},{10,11},{12,13},{... | collective-permute-start | bytes 73736 | tf_op jit(solution)/shard_map/ppermute | solution.py:20
  6.0 12.8 %collective-permute-start.5 = (f32[8,3,2,128]{3,2,1,0:T(2,128)S(1)}, f32[8,3,2,128]{3,2,1,0:T(2,128)S(1)}, u32[]{:S(2)}, u32[]{:S(2)}) collective-permute-start(f32[8,3,2,128]{3,2,1,0:T(2,128)S(1)} %get-tuple-element.197), channel_id=1, source_target_pairs={{1,0},{2,1},{3,2},{5,4},{6,5},{7,6},{9,8},{10,9},{11,10},{13,12},{... | collective-permute-start | bytes 73736 | tf_op jit(solution)/shard_map/ppermute | solution.py:22
  8.0 7.5 %collective-permute-start.2 = (f32[1,1,2,1024]{3,2,1,0:T(2,128)S(1)}, f32[1,1,2,1024]{3,2,1,0:T(2,128)S(1)}, u32[]{:S(2)}, u32[]{:S(2)}) collective-permute-start(f32[1,1,2,1024]{3,2,1,0:T(2,128)S(1)} %get-tuple-element.198), channel_id=1, source_target_pairs={{0,1},{1,2},{2,3},{4,5},{5,6},{6,7},{8,9},{9,10},{10,11},{12,13},{... | collective-permute-start | bytes 24584 | tf_op jit(solution)/shard_map/ppermute | solution.py:20
  12.6 5.5 %collective-permute-start.3 = (f32[1,1,2,1024]{3,2,1,0:T(2,128)S(1)}, f32[1,1,2,1024]{3,2,1,0:T(2,128)S(1)}, u32[]{:S(2)}, u32[]{:S(2)}) collective-permute-start(f32[1,1,2,1024]{3,2,1,0:T(2,128)S(1)} %get-tuple-element.199), channel_id=1, source_target_pairs={{1,0},{2,1},{3,2},{5,4},{6,5},{7,6},{9,8},{10,9},{11,10},{13,12},{... | collective-permute-start | bytes 24584 | tf_op jit(solution)/shard_map/ppermute | solution.py:22
  18.9 20.7 %copy-start.6 = (f32[8,3,12,128]{3,2,1,0:T(8,128)}, f32[8,3,12,128]{3,2,1,0:T(8,128)S(1)}, u32[]{:S(2)}) copy-start(f32[8,3,12,128]{3,2,1,0:T(8,128)S(1)} %get-tuple-element.401) | copy-start | bytes 442372 | tf_op jit(solution)/shard_map/while
  19.2 24.3 %collective-permute-start = (f32[16,3,2,1024]{3,2,0,1:T(2,128)S(1)}, f32[16,3,2,1024]{3,2,0,1:T(2,128)S(1)}, u32[]{:S(2)}, u32[]{:S(2)}) collective-permute-start(f32[16,3,2,1024]{3,2,0,1:T(2,128)S(1)} %get-tuple-element.307), channel_id=1, source_target_pairs={{1,0},{2,1},{3,2},{5,4},{6,5},{7,6},{9,8},{10,9},{11,10},{13,12},{... | collective-permute-start | bytes 1179656 | tf_op jit(solution)/shard_map/while/body/eval_jaxpr/ppermute | solution.py:22
  20.5 23.0 %collective-permute-start.1 = (f32[16,3,2,1024]{3,2,0,1:T(2,128)S(1)}, f32[16,3,2,1024]{3,2,0,1:T(2,128)}, u32[]{:S(2)}, u32[]{:S(2)}) collective-permute-start(f32[16,3,2,1024]{3,2,0,1:T(2,128)S(1)} %get-tuple-element.308), channel_id=1, source_target_pairs={{0,1},{1,2},{2,3},{4,5},{5,6},{6,7},{8,9},{9,10},{10,11},{12,13},{... | collective-permute-start | bytes 1179656 | tf_op jit(solution)/shard_map/while/body/eval_jaxpr/ppermute | solution.py:20
  58.7 20.6 %copy-start.6 = (f32[8,3,12,128]{3,2,1,0:T(8,128)}, f32[8,3,12,128]{3,2,1,0:T(8,128)S(1)}, u32[]{:S(2)}) copy-start(f32[8,3,12,128]{3,2,1,0:T(8,128)S(1)} %get-tuple-element.401) | copy-start | bytes 442372 | tf_op jit(solution)/shard_map/while
  59.0 24.3 %collective-permute-start = (f32[16,3,2,1024]{3,2,0,1:T(2,128)S(1)}, f32[16,3,2,1024]{3,2,0,1:T(2,128)S(1)}, u32[]{:S(2)}, u32[]{:S(2)}) collective-permute-start(f32[16,3,2,1024]{3,2,0,1:T(2,128)S(1)} %get-tuple-element.307), channel_id=1, source_target_pairs={{1,0},{2,1},{3,2},{5,4},{6,5},{7,6},{9,8},{10,9},{11,10},{13,12},{... | collective-permute-start | bytes 1179656 | tf_op jit(solution)/shard_map/while/body/eval_jaxpr/ppermute | solution.py:22
  60.3 23.0 %collective-permute-start.1 = (f32[16,3,2,1024]{3,2,0,1:T(2,128)S(1)}, f32[16,3,2,1024]{3,2,0,1:T(2,128)}, u32[]{:S(2)}, u32[]{:S(2)}) collective-permute-start(f32[16,3,2,1024]{3,2,0,1:T(2,128)S(1)} %get-tuple-element.308), channel_id=1, source_target_pairs={{0,1},{1,2},{2,3},{4,5},{5,6},{6,7},{8,9},{9,10},{10,11},{12,13},{... | collective-permute-start | bytes 1179656 | tf_op jit(solution)/shard_map/while/body/eval_jaxpr/ppermute | solution.py:20
  98.9 23.4 %collective-permute-start = (f32[16,3,2,1024]{3,2,0,1:T(2,128)S(1)}, f32[16,3,2,1024]{3,2,0,1:T(2,128)S(1)}, u32[]{:S(2)}, u32[]{:S(2)}) collective-permute-start(f32[16,3,2,1024]{3,2,0,1:T(2,128)S(1)} %get-tuple-element.307), channel_id=1, source_target_pairs={{1,0},{2,1},{3,2},{5,4},{6,5},{7,6},{9,8},{10,9},{11,10},{13,12},{... | collective-permute-start | bytes 1179656 | tf_op jit(solution)/shard_map/while/body/eval_jaxpr/ppermute | solution.py:22
  100.2 22.1 %collective-permute-start.1 = (f32[16,3,2,1024]{3,2,0,1:T(2,128)S(1)}, f32[16,3,2,1024]{3,2,0,1:T(2,128)}, u32[]{:S(2)}, u32[]{:S(2)}) collective-permute-start(f32[16,3,2,1024]{3,2,0,1:T(2,128)S(1)} %get-tuple-element.308), channel_id=1, source_target_pairs={{0,1},{1,2},{2,3},{4,5},{5,6},{6,7},{8,9},{9,10},{10,11},{12,13},{... | collective-permute-start | bytes 1179656 | tf_op jit(solution)/shard_map/while/body/eval_jaxpr/ppermute | solution.py:20
  137.4 20.6 %copy-start.6 = (f32[8,3,12,128]{3,2,1,0:T(8,128)}, f32[8,3,12,128]{3,2,1,0:T(8,128)S(1)}, u32[]{:S(2)}) copy-start(f32[8,3,12,128]{3,2,1,0:T(8,128)S(1)} %get-tuple-element.401) | copy-start | bytes 442372 | tf_op jit(solution)/shard_map/while
  137.7 24.3 %collective-permute-start = (f32[16,3,2,1024]{3,2,0,1:T(2,128)S(1)}, f32[16,3,2,1024]{3,2,0,1:T(2,128)S(1)}, u32[]{:S(2)}, u32[]{:S(2)}) collective-permute-start(f32[16,3,2,1024]{3,2,0,1:T(2,128)S(1)} %get-tuple-element.307), channel_id=1, source_target_pairs={{1,0},{2,1},{3,2},{5,4},{6,5},{7,6},{9,8},{10,9},{11,10},{13,12},{... | collective-permute-start | bytes 1179656 | tf_op jit(solution)/shard_map/while/body/eval_jaxpr/ppermute | solution.py:22
  139.0 23.0 %collective-permute-start.1 = (f32[16,3,2,1024]{3,2,0,1:T(2,128)S(1)}, f32[16,3,2,1024]{3,2,0,1:T(2,128)}, u32[]{:S(2)}, u32[]{:S(2)}) collective-permute-start(f32[16,3,2,1024]{3,2,0,1:T(2,128)S(1)} %get-tuple-element.308), channel_id=1, source_target_pairs={{0,1},{1,2},{2,3},{4,5},{5,6},{6,7},{8,9},{9,10},{10,11},{12,13},{... | collective-permute-start | bytes 1179656 | tf_op jit(solution)/shard_map/while/body/eval_jaxpr/ppermute | solution.py:20
  177.6 23.4 %collective-permute-start = (f32[16,3,2,1024]{3,2,0,1:T(2,128)S(1)}, f32[16,3,2,1024]{3,2,0,1:T(2,128)S(1)}, u32[]{:S(2)}, u32[]{:S(2)}) collective-permute-start(f32[16,3,2,1024]{3,2,0,1:T(2,128)S(1)} %get-tuple-element.307), channel_id=1, source_target_pairs={{1,0},{2,1},{3,2},{5,4},{6,5},{7,6},{9,8},{10,9},{11,10},{13,12},{... | collective-permute-start | bytes 1179656 | tf_op jit(solution)/shard_map/while/body/eval_jaxpr/ppermute | solution.py:22
  178.9 22.1 %collective-permute-start.1 = (f32[16,3,2,1024]{3,2,0,1:T(2,128)S(1)}, f32[16,3,2,1024]{3,2,0,1:T(2,128)}, u32[]{:S(2)}, u32[]{:S(2)}) collective-permute-start(f32[16,3,2,1024]{3,2,0,1:T(2,128)S(1)} %get-tuple-element.308), channel_id=1, source_target_pairs={{0,1},{1,2},{2,3},{4,5},{5,6},{6,7},{8,9},{9,10},{10,11},{12,13},{... | collective-permute-start | bytes 1179656 | tf_op jit(solution)/shard_map/while/body/eval_jaxpr/ppermute | solution.py:20
  216.5 24.3 %collective-permute-start = (f32[16,3,2,1024]{3,2,0,1:T(2,128)S(1)}, f32[16,3,2,1024]{3,2,0,1:T(2,128)S(1)}, u32[]{:S(2)}, u32[]{:S(2)}) collective-permute-start(f32[16,3,2,1024]{3,2,0,1:T(2,128)S(1)} %get-tuple-element.307), channel_id=1, source_target_pairs={{1,0},{2,1},{3,2},{5,4},{6,5},{7,6},{9,8},{10,9},{11,10},{13,12},{... | collective-permute-start | bytes 1179656 | tf_op jit(solution)/shard_map/while/body/eval_jaxpr/ppermute | solution.py:22
  217.8 23.0 %collective-permute-start.1 = (f32[16,3,2,1024]{3,2,0,1:T(2,128)S(1)}, f32[16,3,2,1024]{3,2,0,1:T(2,128)}, u32[]{:S(2)}, u32[]{:S(2)}) collective-permute-start(f32[16,3,2,1024]{3,2,0,1:T(2,128)S(1)} %get-tuple-element.308), channel_id=1, source_target_pairs={{0,1},{1,2},{2,3},{4,5},{5,6},{6,7},{8,9},{9,10},{10,11},{12,13},{... | collective-permute-start | bytes 1179656 | tf_op jit(solution)/shard_map/while/body/eval_jaxpr/ppermute | solution.py:20
  256.3 23.4 %collective-permute-start = (f32[16,3,2,1024]{3,2,0,1:T(2,128)S(1)}, f32[16,3,2,1024]{3,2,0,1:T(2,128)S(1)}, u32[]{:S(2)}, u32[]{:S(2)}) collective-permute-start(f32[16,3,2,1024]{3,2,0,1:T(2,128)S(1)} %get-tuple-element.307), channel_id=1, source_target_pairs={{1,0},{2,1},{3,2},{5,4},{6,5},{7,6},{9,8},{10,9},{11,10},{13,12},{... | collective-permute-start | bytes 1179656 | tf_op jit(solution)/shard_map/while/body/eval_jaxpr/ppermute | solution.py:22
  257.6 22.1 %collective-permute-start.1 = (f32[16,3,2,1024]{3,2,0,1:T(2,128)S(1)}, f32[16,3,2,1024]{3,2,0,1:T(2,128)}, u32[]{:S(2)}, u32[]{:S(2)}) collective-permute-start(f32[16,3,2,1024]{3,2,0,1:T(2,128)S(1)} %get-tuple-element.308), channel_id=1, source_target_pairs={{0,1},{1,2},{2,3},{4,5},{5,6},{6,7},{8,9},{9,10},{10,11},{12,13},{... | collective-permute-start | bytes 1179656 | tf_op jit(solution)/shard_map/while/body/eval_jaxpr/ppermute | solution.py:20
  295.2 24.3 %collective-permute-start = (f32[16,3,2,1024]{3,2,0,1:T(2,128)S(1)}, f32[16,3,2,1024]{3,2,0,1:T(2,128)S(1)}, u32[]{:S(2)}, u32[]{:S(2)}) collective-permute-start(f32[16,3,2,1024]{3,2,0,1:T(2,128)S(1)} %get-tuple-element.307), channel_id=1, source_target_pairs={{1,0},{2,1},{3,2},{5,4},{6,5},{7,6},{9,8},{10,9},{11,10},{13,12},{... | collective-permute-start | bytes 1179656 | tf_op jit(solution)/shard_map/while/body/eval_jaxpr/ppermute | solution.py:22
  296.5 23.0 %collective-permute-start.1 = (f32[16,3,2,1024]{3,2,0,1:T(2,128)S(1)}, f32[16,3,2,1024]{3,2,0,1:T(2,128)}, u32[]{:S(2)}, u32[]{:S(2)}) collective-permute-start(f32[16,3,2,1024]{3,2,0,1:T(2,128)S(1)} %get-tuple-element.308), channel_id=1, source_target_pairs={{0,1},{1,2},{2,3},{4,5},{5,6},{6,7},{8,9},{9,10},{10,11},{12,13},{... | collective-permute-start | bytes 1179656 | tf_op jit(solution)/shard_map/while/body/eval_jaxpr/ppermute | solution.py:20
  352.1 24.5 %all-to-all-start = ((f32[8,1,49152]{2,1,0:T(1,128)}), f32[8,1,49152]{2,1,0:T(1,128)S(1)}, u32[]{:S(2)}, u32[]{:S(2)}) async-start(f32[8,1,49152]{2,1,0:T(1,128)} %reshape.42), calls=%async_computation | async-start | bytes 3145728 | tf_op jit(solution)/shard_map/all_to_all | solution.py:109
  (72 other events, 195.3 us)
where the time goes:
time: 406 us; the launch traced here: 402 us
  other arithmetic  119 us (29%)
  local copies, waits for them, and re-layouts  97 us (24%)
  blocking collectives  73.6 us (18%)
  starting transfers between devices  68.4 us (17%)
  waiting for transfers between devices  23.5 us (6%)
  loops' own time  19.3 us (5%)
    all_gather x8, blocking collectives, fetch_flow(): return lax.all_gather(held_tile, 'mode', axis=2, tiled=True)  73.6 us
    another operation x56, other arithmetic, tendency(): return jnp.stack([height_rate, zonal_rate, merid_rate], 1)  53.8 us
    ppermute x10, starting transfers between devices, padded(): lax.ppermute(tail, axis, [(i, (i + 1) % count) for i in range(ends)])  51.9 us
    slice x144, local copies, waits for them, and re-layouts, deriv_x(): return 0.5 * (jnp.roll(values, -1, -1) - jnp.roll(values, 1, -1))  37.2 us
    mul x32, other arithmetic, deriv_x(): return 0.5 * (jnp.roll(values, -1, -1) - jnp.roll(values, 1, -1))  24.6 us
    all_to_all x1, waiting for transfers between devices, on_device(): lax.all_to_all(final, 'mode', split_axis=3, concat_axis=0, tiled=True)  20.9 us
    another operation x1, loops' own time, on_device(): final = lax.fori_loop(0, total_steps, advance, current)  19.3 us
    unnamed x8, local copies, waits for them, and re-layouts  18.9 us
  transfers between devices with their start and end apart: 21, of which 2 were waited for; matrix products, arithmetic and copies ran while one was open for 13% of the time, Pallas kernels for 0%

commit v1 on v0

--- a/solution.py
+++ b/solution.py
@@ -1,6 +1,10 @@
+import functools
+
 import jax
 import jax.numpy as jnp
 from jax import lax
+from jax.experimental import pallas as pl
+from jax.experimental.pallas import tpu as pltpu
 from jax.sharding import PartitionSpec as P
 
 mean_depth = 1.0
@@ -84,7 +88,7 @@
     )
 
 
-def on_device(tangents, checkpoints, owner_order, land_mask, coefficients):
+def on_device_general(tangents, checkpoints, owner_order, land_mask, coefficients):
     wet_mask = land_mask.astype(jnp.float32)
     current = wet_mask * tangents
     depth = 2
@@ -112,6 +116,231 @@
         mixing.T, flattened, precision=lax.Precision.HIGHEST, preferred_element_type=jnp.float32
     )
     return mixed.reshape(cell_block.shape)
+
+
+LANES = 128
+SUB = 8
+COEFS = 7
+
+
+def tile_shift(values, lane, ahead):
+    tiles = values.shape[0]
+    if ahead:
+        rolled = pltpu.roll(values, LANES - 1, 2)
+        beside = jnp.concatenate([rolled[1:], rolled[:1]], axis=0) if tiles > 1 else rolled
+        return jnp.where(lane == LANES - 1, beside, rolled)
+    rolled = pltpu.roll(values, 1, 2)
+    beside = jnp.concatenate([rolled[-1:], rolled[:-1]], axis=0) if tiles > 1 else rolled
+    return jnp.where(lane == 0, beside, rolled)
+
+
+def diff_x(values, lane):
+    return tile_shift(values, lane, True) - tile_shift(values, lane, False)
+
+
+def zero_pads(ref, strips):
+    lead = ref.shape[:-2]
+    edge = jnp.zeros(lead + (SUB, LANES), jnp.float32)
+    ref[..., pl.ds(0, SUB), :] = edge
+    ref[..., pl.ds(SUB * (strips + 1), SUB), :] = edge
+
+
+def band(strip, shift=0):
+    return pl.ds(SUB * (strip + 1) + shift, SUB)
+
+
+def build_coefs(order, base_ref, coef, flow_pad, strips, steps, lane):
+    zero_pads(flow_pad, strips)
+
+    def one(step, carry):
+        slot = order[step]
+        for strip in range(strips):
+            cells = base_ref[:, strip, slot]
+            coef[step, 0, :, pl.ds(SUB * strip, SUB), :] = 0.0625 * (mean_depth + cells[:, 0])
+            flow_pad[0, :, band(strip), :] = 0.25 * cells[:, 1]
+            flow_pad[1, :, band(strip), :] = 0.25 * cells[:, 2]
+        for strip in range(strips):
+            rows = pl.ds(SUB * strip, SUB)
+            flow_u = flow_pad[0, :, band(strip), :]
+            flow_v = flow_pad[1, :, band(strip), :]
+            coef[step, 1, :, rows, :] = flow_u
+            coef[step, 2, :, rows, :] = flow_v
+            coef[step, 3, :, rows, :] = diff_x(flow_u, lane)
+            coef[step, 4, :, rows, :] = 0.25 - (
+                flow_pad[0, :, band(strip, 1), :] - flow_pad[0, :, band(strip, -1), :]
+            )
+            coef[step, 5, :, rows, :] = 0.25 + diff_x(flow_v, lane)
+            coef[step, 6, :, rows, :] = (
+                flow_pad[1, :, band(strip, 1), :] - flow_pad[1, :, band(strip, -1), :]
+            )
+        return carry
+
+    lax.fori_loop(0, steps, one, 0)
+
+
+def store_flux(source, flux, coef, step, strip):
+    rows = pl.ds(SUB * strip, SUB)
+    flux[:, band(strip), :] = (
+        coef[step, 0, :, rows, :] * source[2, :, band(strip), :]
+        + coef[step, 2, :, rows, :] * source[0, :, band(strip), :]
+    )
+
+
+def scaled_rates(source, flux, coef, step, strip, lane):
+    rows = pl.ds(SUB * strip, SUB)
+    here, above, below = band(strip), band(strip, 1), band(strip, -1)
+    height, zonal, merid = source[0, :, here, :], source[1, :, here, :], source[2, :, here, :]
+    depth, flow_u, flow_v, du_dx, turn_v, turn_u, dv_dy = (
+        coef[step, i, :, rows, :] for i in range(COEFS)
+    )
+    flux_x = depth * zonal + flow_u * height
+    rate_h = diff_x(flux_x, lane) + (flux[:, above, :] - flux[:, below, :])
+    rate_u = turn_v * merid - (
+        flow_u * diff_x(zonal, lane)
+        + du_dx * zonal
+        + flow_v * (source[1, :, above, :] - source[1, :, below, :])
+        + diff_x(height, lane)
+    )
+    rate_v = (
+        flow_u * diff_x(merid, lane)
+        + turn_u * zonal
+        + flow_v * (source[2, :, above, :] - source[2, :, below, :])
+        + dv_dy * merid
+        + (source[0, :, above, :] - source[0, :, below, :])
+    )
+    return (height, zonal, merid), (-rate_h, rate_u, -rate_v)
+
+
+def run_steps(state, middle, flux, coef, wet, strips, steps, lane):
+    def one(step, carry):
+        for strip in range(strips):
+            store_flux(state, flux, coef, step, strip)
+        for strip in range(strips):
+            held, rates = scaled_rates(state, flux, coef, step, strip, lane)
+            water = wet[:, pl.ds(SUB * strip, SUB), :]
+            for f in range(3):
+                middle[f, :, band(strip), :] = water * (held[f] + rates[f])
+        for strip in range(strips):
+            store_flux(middle, flux, coef, step, strip)
+        for strip in range(strips):
+            held, rates = scaled_rates(middle, flux, coef, step, strip, lane)
+            water = wet[:, pl.ds(SUB * strip, SUB), :]
+            for f in range(3):
+                state[f, :, band(strip), :] = state[f, :, band(strip), :] + water * (
+                    held[f] + rates[f]
+                )
+        return carry
+
+    lax.fori_loop(0, steps, one, 0)
+
+
+def steps_kernel(strips, steps, tiles, order, tan_ref, base_ref, land_ref, out_ref,
+                 coef, wet, state, middle, flux, flow_pad):
+    lane = lax.broadcasted_iota(jnp.int32, (tiles, SUB, LANES), 2)
+
+    @pl.when(pl.program_id(0) == 0)
+    def _():
+        for ref in (state, middle, flux):
+            zero_pads(ref, strips)
+        for strip in range(strips):
+            for t in range(tiles):
+                wet[t, pl.ds(SUB * strip, SUB), :] = land_ref[
+                    strip, :, pl.ds(LANES * t, LANES)
+                ].astype(jnp.float32)
+        build_coefs(order, base_ref, coef, flow_pad, strips, steps, lane)
+
+    for f, scale in enumerate((0.25, 1.0, 1.0)):
+        for strip in range(strips):
+            for t in range(tiles):
+                state[f, t, band(strip), :] = (
+                    scale * wet[t, pl.ds(SUB * strip, SUB), :]
+                ) * tan_ref[strip, 0, f, :, pl.ds(LANES * t, LANES)]
+    run_steps(state, middle, flux, coef, wet, strips, steps, lane)
+    down = 0.5 ** steps
+    for f, scale in enumerate((4.0 * down, down, down)):
+        for strip in range(strips):
+            out_ref[:, strip, 0, f] = scale * state[f, :, band(strip), :]
+
+
+def step_modes(order, tangents, base, land):
+    strips, modes, fields, rows, columns = tangents.shape
+    tiles, _, steps = base.shape[:3]
+    tall = SUB * (strips + 2)
+    return pl.pallas_call(
+        functools.partial(steps_kernel, strips, steps, tiles),
+        out_shape=jax.ShapeDtypeStruct((tiles, strips, modes, fields, rows, LANES), jnp.float32),
+        grid_spec=pltpu.PrefetchScalarGridSpec(
+            num_scalar_prefetch=1,
+            grid=(modes,),
+            in_specs=[
+                pl.BlockSpec((strips, 1, fields, rows, columns), lambda k, o: (0, k, 0, 0, 0)),
+                pl.BlockSpec(base.shape, lambda k, o: (0,) * 6, pipeline_mode=pl.Buffered(1)),
+                pl.BlockSpec(land.shape, lambda k, o: (0,) * 3, pipeline_mode=pl.Buffered(1)),
+            ],
+            out_specs=pl.BlockSpec(
+                (tiles, strips, 1, fields, rows, LANES), lambda k, o: (0, 0, k, 0, 0, 0)
+            ),
+            scratch_shapes=[
+                pltpu.VMEM((steps, COEFS, tiles, SUB * strips, LANES), jnp.float32),
+                pltpu.VMEM((tiles, SUB * strips, LANES), jnp.float32),
+                pltpu.VMEM((3, tiles, tall, LANES), jnp.float32),
+                pltpu.VMEM((3, tiles, tall, LANES), jnp.float32),
+                pltpu.VMEM((tiles, tall, LANES), jnp.float32),
+                pltpu.VMEM((2, tiles, tall, LANES), jnp.float32),
+            ],
+        ),
+    )(order, tangents, base, land)
+
+
+def mix_kernel(coef_ref, cells_ref, out_ref):
+    modes = coef_ref.shape[0]
+    row = lax.broadcasted_iota(jnp.int32, (modes, modes), 0)
+    col = lax.broadcasted_iota(jnp.int32, (modes, modes), 1)
+    mixing = jnp.where(row <= col, coef_ref[...], 0.0) + jnp.where(row == col, 1.0, 0.0)
+    turned = mixing.T
+    per = cells_ref.shape[0] // modes
+    for spot in range(per):
+        cells = cells_ref[pl.ds(spot, modes, stride=per), :]
+        out_ref[pl.ds(spot, modes, stride=per), :] = jnp.dot(
+            turned, cells, precision=lax.Precision.HIGHEST, preferred_element_type=jnp.float32
+        )
+
+
+def mix(coefficients, cells):
+    return pl.pallas_call(
+        mix_kernel,
+        out_shape=jax.ShapeDtypeStruct(cells.shape, jnp.float32),
+        in_specs=[pl.BlockSpec(memory_space=pltpu.VMEM)] * 2,
+        out_specs=pl.BlockSpec(memory_space=pltpu.VMEM),
+    )(coefficients, cells)
+
+
+def on_device_whole(tangents, checkpoints, owner_order, land_mask, coefficients):
+    strips = lax.axis_size("rows")
+    tiles = lax.axis_size("mode")
+    held, fields, rows, columns = tangents.shape
+    steps = checkpoints.shape[0]
+    base = lax.all_gather(checkpoints, ("mode", "rows"))
+    base = base.reshape(tiles, strips, steps, fields, rows, LANES)
+    land = lax.all_gather(land_mask, "rows")
+    whole = lax.all_to_all(tangents, "rows", split_axis=0, concat_axis=0, tiled=True)
+    whole = whole.reshape(strips, held // strips, fields, rows, columns)
+    done = step_modes(owner_order, whole, base, land)
+    done = done.reshape(tiles * strips, held // strips * fields * rows, LANES)
+    placed = lax.all_to_all(done, ("mode", "rows"), split_axis=0, concat_axis=0, tiled=True)
+    mixed = mix(coefficients, placed.reshape(-1, LANES))
+    return mixed.reshape(coefficients.shape[0], fields, rows, LANES)
+
+
+def on_device(tangents, checkpoints, owner_order, land_mask, coefficients):
+    strips = lax.axis_size("rows")
+    held, _, rows, columns = tangents.shape
+    fits = (
+        held % strips == 0 and rows == SUB and checkpoints.shape[-1] == LANES and strips <= 8
+        and coefficients.shape[0] % LANES == 0
+    )
+    chosen = on_device_whole if fits else on_device_general
+    return chosen(tangents, checkpoints, owner_order, land_mask, coefficients)
 
 
 def solution(mesh):

time: 406 us -> 165 us (0.41)
  other arithmetic: 119 us -> 0 us
  local copies, waits for them, and re-layouts: 97 us -> 0.01 us
  starting transfers between devices: 68.4 us -> 6.36 us
  Pallas kernels: 0 us -> 32.2 us
  loops' own time: 19.3 us -> 0 us
  blocking collectives: 73.6 us -> 88 us
  between operations: 0.16 us -> 13.4 us
    ppermute x20 -> x0, starting transfers between devices: 64.8 us -> none  [the longest x10 51.9 us: padded(): lax.ppermute(tail, axis, [(i, (i + 1) % count) for i in range(ends)])]
    another operation x56 -> x0, other arithmetic: 53.8 us -> none  [tendency(): return jnp.stack([height_rate, zonal_rate, merid_rate], 1)]
    slice x170 -> x0, local copies, waits for them, and re-layouts: 45.4 us -> none  [the longest x144 37.2 us: deriv_x(): return 0.5 * (jnp.roll(values, -1, -1) - jnp.roll(values, 1, -1))]
    all_to_all x0 -> x1, blocking collectives: none -> 40.2 us  [on_device_whole(): lax.all_to_all(done, ('mode', 'rows'), split_axis=0, concat_axis=0, tiled...]
    mul x73 -> x0, other arithmetic: 39.7 us -> none  [the longest x32 24.6 us: deriv_x(): return 0.5 * (jnp.roll(values, -1, -1) - jnp.roll(values, 1, -1))]
    pallas_call x0 -> x2, Pallas kernels: none -> 32.2 us  [the longest x1 28.1 us: step_modes(): pl.pallas_call(functools.partial(steps_kernel, strips, steps, tiles), out...]
    all_gather x8 -> x1, blocking collectives: 73.6 us -> 47.8 us  [on_device_whole(): land = lax.all_gather(land_mask, 'rows')]
    all_gather x0 -> x1, waiting for transfers between devices: none -> 23 us  [on_device_whole(): base = lax.all_gather(checkpoints, ('mode', 'rows'))]
  transfers between devices with their start and end apart: 21 -> 2, of which waited for: 2 -> 1; matrix products, arithmetic and copies ran while one was open for 13% -> 0% of each run, Pallas kernels for 0% -> 0%
where the time goes in v1:
time: 165 us; the launch traced here: 164 us
  blocking collectives  88 us (53%)
  Pallas kernels  32.2 us (20%)
  waiting for transfers between devices  23.8 us (14%)
  between operations  13.4 us (8%)
  starting transfers between devices  6.36 us (4%)
    all_gather x1, blocking collectives, on_device_whole(): land = lax.all_gather(land_mask, 'rows')  47.8 us
    all_to_all x1, blocking collectives, on_device_whole(): lax.all_to_all(done, ('mode', 'rows'), split_axis=0, concat_axis=0, tiled...  40.2 us
    pallas_call x1, Pallas kernels, step_modes(): pl.pallas_call(functools.partial(steps_kernel, strips, steps, tiles), out...  28.1 us
    all_gather x1, waiting for transfers between devices, on_device_whole(): base = lax.all_gather(checkpoints, ('mode', 'rows'))  23 us
    all_to_all x1, starting transfers between devices, on_device_whole(): lax.all_to_all(tangents, 'rows', split_axis=0, concat_axis=0, tiled=True)  6.36 us
    pallas_call x1, Pallas kernels, mix(): pl.pallas_call(mix_kernel, out_shape=jax.ShapeDtypeStruct(cells.shape, jn...  4.17 us
  transfers between devices with their start and end apart: 2, of which 1 were waited for; matrix products, arithmetic and copies ran while one was open for 0% of the time, Pallas kernels for 0%

profile of v1, /device:TPU:0, one launch (start us, length us, event | category | flops | bytes accessed | tf_op | source)
XLA Modules:
  0.0 163.7 jit_solution(2567526096347633703)
XLA Ops:
  6.5 0.0 all-gather.4.cloned.1.call-start
  6.5 0.7 all-gather.4.cloned.1.call-update
  7.3 0.0 copy-start.1
  7.3 6.4 %all-to-all-start = ((f32[16,3,8,1024]{3,2,1,0:T(8,128)}), f32[16,3,8,1024]{3,2,1,0:T(8,128)S(1)}, u32[]{:S(2)}, u32[]{:S(2)}) async-start(f32[16,3,8,1024]{3,2,1,0:T(8,128)} %param.5), calls=%async_computation | async-start | bytes 3145728 | tf_op jit(solution)/shard_map/all_to_all | solution.py:326
  13.6 0.0 copy-done.1
  13.6 47.8 %all-gather.1 = s32[32,1024]{1,0:T(8,128)} all-gather(s32[8,1024]{1,0:T(8,128)S(1)} %copy-done.1), channel_id=3, replica_groups=mesh['mode'=8,'rows'=4] {'rows'}, dimensions={0}, use_global_device_ids=true | all-gather | bytes 163840 | tf_op jit(solution)/shard_map/all_gather | solution.py:325
  61.4 0.0 all-to-all-done
  61.4 0.0 copy-start
  61.4 23.0 %all-gather.4.cloned.1.call-done = f32[256,3,8,128]{3,2,1,0:T(8,128)} async-done(((f32[8,3,8,128]{3,2,1,0:T(8,128)}), f32[256,3,8,128]{3,2,1,0:T(8,128)}) %all-gather.4.cloned.1.call-update) | async-done | bytes 3145744 | tf_op jit(solution)/shard_map/all_gather | solution.py:323
  84.5 0.0 copy-done
  84.5 28.1 %shard_map.55 = f32[8,4,4,3,8,128]{5,4,3,2,1,0:T(8,128)} custom-call(s32[8]{0:T(128)} %order.1, f32[4,4,3,8,1024]{4,3,2,1,0:T(8,128)} %bitcast.7, f32[8,4,8,3,8,128]{5,4,3,2,1,0:T(8,128)} %bitcast.9, s32[4,8,1024]{2,1,0:T(8,128)} %bitcast.10), custom_call_target="tpu_custom_call" | custom-call | tf_op jit(solution)/shard_map/pallas_call | solution.py:269
  112.6 40.2 %all_to_all.10 = f32[32,96,128]{2,1,0:T(8,128)} all-to-all(f32[32,96,128]{2,1,0:T(8,128)} %bitcast.8), channel_id=1, replica_groups=mesh['mode'=8,'rows'=4] {'mode','rows'}, dimensions={0} | all-to-all | bytes 3145728 | tf_op jit(solution)/shard_map/all_to_all | solution.py:330
  152.7 4.2 %shard_map.56 = f32[3072,128]{1,0:T(8,128)} custom-call(f32[128,128]{1,0:T(8,128)} %coef_ref.1, f32[3072,128]{1,0:T(8,128)} %bitcast.6), custom_call_target="tpu_custom_call" | custom-call | tf_op jit(solution)/shard_map/pallas_call | solution.py:310
Async XLA Ops:
  6.5 78.0 %all-gather.4.cloned.1.call-start = ((), (), s32[]{:S(2)}) async-start(), calls=%async_computation.2 | async-start | bytes 3244032 | tf_op jit(solution)/shard_map/all_gather | solution.py:323
  7.3 6.4 %copy-start.1 = (s32[8,1024]{1,0:T(8,128)S(1)}, s32[8,1024]{1,0:T(8,128)}, u32[]{:S(2)}) copy-start(s32[8,1024]{1,0:T(8,128)} %param.8) | copy-start | bytes 98308
  7.3 54.2 %all-to-all-start = ((f32[16,3,8,1024]{3,2,1,0:T(8,128)}), f32[16,3,8,1024]{3,2,1,0:T(8,128)S(1)}, u32[]{:S(2)}, u32[]{:S(2)}) async-start(f32[16,3,8,1024]{3,2,1,0:T(8,128)} %param.5), calls=%async_computation | async-start | bytes 3145728 | tf_op jit(solution)/shard_map/all_to_all | solution.py:326
  61.4 23.1 %copy-start = (f32[16,3,8,1024]{3,2,1,0:T(8,128)}, f32[16,3,8,1024]{3,2,1,0:T(8,128)S(1)}, u32[]{:S(2)}) copy-start(f32[16,3,8,1024]{3,2,1,0:T(8,128)S(1)} %all-to-all-done) | copy-start | bytes 4718596
Sparse Core Ops, SparseCore 0:
  10.2 74.2 all-gather.3

commit v2 on v1

--- a/solution.py
+++ b/solution.py
@@ -153,12 +153,13 @@
     zero_pads(flow_pad, strips)
 
     def one(step, carry):
-        slot = order[step]
-        for strip in range(strips):
-            cells = base_ref[:, strip, slot]
-            coef[step, 0, :, pl.ds(SUB * strip, SUB), :] = 0.0625 * (mean_depth + cells[:, 0])
-            flow_pad[0, :, band(strip), :] = 0.25 * cells[:, 1]
-            flow_pad[1, :, band(strip), :] = 0.25 * cells[:, 2]
+        first = 3 * order[step]
+        for strip in range(strips):
+            coef[step, 0, :, pl.ds(SUB * strip, SUB), :] = 0.0625 * (
+                mean_depth + base_ref[:, strip, first]
+            )
+            flow_pad[0, :, band(strip), :] = 0.25 * base_ref[:, strip, first + 1]
+            flow_pad[1, :, band(strip), :] = 0.25 * base_ref[:, strip, first + 2]
         for strip in range(strips):
             rows = pl.ds(SUB * strip, SUB)
             flow_u = flow_pad[0, :, band(strip), :]
@@ -234,62 +235,147 @@
     lax.fori_loop(0, steps, one, 0)
 
 
-def steps_kernel(strips, steps, tiles, order, tan_ref, base_ref, land_ref, out_ref,
-                 coef, wet, state, middle, flux, flow_pad):
+def steps_kernel(strips, tiles, steps, kept, order, base_ref, land_ref, tan_ref, out_ref,
+                 base_all, whole, leaving, coef, wet, state, middle, flux, flow_pad,
+                 z_send, z_recv, x_send, x_recv, p_send, p_recv,
+                 in_send, in_recv, out_send, out_recv):
+    m = lax.axis_index("mode")
+    r = lax.axis_index("rows")
+    everyone = tiles * strips
+    me = m * strips + r
+    chips = tiles // 2
+    pairs = 2 * (m // 2)
+    core = m - pairs
+    partner = pairs + 1 - core
+    mask_at = 3 * steps
     lane = lax.broadcasted_iota(jnp.int32, (tiles, SUB, LANES), 2)
 
-    @pl.when(pl.program_id(0) == 0)
-    def _():
-        for ref in (state, middle, flux):
-            zero_pads(ref, strips)
-        for strip in range(strips):
-            for t in range(tiles):
-                wet[t, pl.ds(SUB * strip, SUB), :] = land_ref[
-                    strip, :, pl.ds(LANES * t, LANES)
-                ].astype(jnp.float32)
-        build_coefs(order, base_ref, coef, flow_pad, strips, steps, lane)
-
-    for f, scale in enumerate((0.25, 1.0, 1.0)):
-        for strip in range(strips):
-            for t in range(tiles):
-                state[f, t, band(strip), :] = (
-                    scale * wet[t, pl.ds(SUB * strip, SUB), :]
-                ) * tan_ref[strip, 0, f, :, pl.ds(LANES * t, LANES)]
-    run_steps(state, middle, flux, coef, wet, strips, steps, lane)
-    down = 0.5 ** steps
-    for f, scale in enumerate((4.0 * down, down, down)):
-        for strip in range(strips):
-            out_ref[:, strip, 0, f] = scale * state[f, :, band(strip), :]
-
-
-def step_modes(order, tangents, base, land):
-    strips, modes, fields, rows, columns = tangents.shape
-    tiles, _, steps = base.shape[:3]
+    def other_chip(j):
+        return lax.rem(m + 2 * j, tiles)
+
+    def send(source, target, sent, received, mode, row):
+        pltpu.make_async_remote_copy(
+            src_ref=source, dst_ref=target, send_sem=sent, recv_sem=received,
+            device_id=(mode, row), device_id_type=pl.DeviceIdType.MESH,
+        ).start()
+
+    def drain(ref, sem):
+        pltpu.make_async_copy(ref, ref, sem).wait()
+
+    barrier = pltpu.get_barrier_semaphore()
+
+    def greet(j, carry):
+        target = lax.rem(me + j, everyone)
+        pl.semaphore_signal(
+            barrier, inc=1, device_id=(target // strips, lax.rem(target, strips)),
+            device_id_type=pl.DeviceIdType.MESH,
+        )
+        return carry
+
+    lax.fori_loop(1, everyone, greet, 0)
+
+    own = base_all.at[m, r]
+    own[pl.ds(0, mask_at)] = base_ref[...].reshape(mask_at, SUB, LANES)
+    own[mask_at] = land_ref[:, pl.ds(pl.multiple_of(m * LANES, LANES), LANES)].astype(jnp.float32)
+
+    pl.semaphore_wait(barrier, everyone - 1)
+
+    for j in range(1, strips):
+        q = lax.rem(r + j, strips)
+        send(own, own, z_send, z_recv.at[r], m, q)
+    for j in range(1, chips):
+        send(own, own, x_send, x_recv.at[m], other_chip(j), r)
+
+    for k in range(kept):
+        for j in range(1, strips):
+            q = lax.rem(r + j, strips)
+            send(tan_ref.at[q * kept + k], whole.at[k, r], in_send, in_recv.at[k], m, q)
+        pltpu.make_async_copy(tan_ref.at[r * kept + k], whole.at[k, r], in_recv.at[k]).start()
+
+    for j in range(1, strips):
+        q = lax.rem(r + j, strips)
+        strip = base_all.at[m, q]
+        drain(strip, z_recv.at[q])
+        for i in range(1, chips):
+            send(strip, strip, x_send, x_recv.at[m], other_chip(i), r)
+    send(base_all.at[m], base_all.at[m], p_send, p_recv, partner, r)
+    for ref in (state, middle, flux):
+        zero_pads(ref, strips)
+    for j in range(1, chips):
+        tile = other_chip(j)
+        drain(base_all.at[tile], x_recv.at[tile])
+        send(base_all.at[tile], base_all.at[tile], p_send, p_recv, partner, r)
+    drain(base_all.at[pl.ds(0, chips)], p_recv)
+
+    for strip in range(strips):
+        wet[:, pl.ds(SUB * strip, SUB), :] = base_all[:, strip, mask_at]
+    build_coefs(order, base_all, coef, flow_pad, strips, steps, lane)
+
+    def one_mode(k, carry):
+        drain(whole.at[k], in_recv.at[k])
+        for f, scale in enumerate((0.25, 1.0, 1.0)):
+            for strip in range(strips):
+                for t in range(tiles):
+                    state[f, t, band(strip), :] = (
+                        scale * wet[t, pl.ds(SUB * strip, SUB), :]
+                    ) * whole[k, strip, f, :, pl.ds(LANES * t, LANES)]
+        run_steps(state, middle, flux, coef, wet, strips, steps, lane)
+        down = 0.5 ** steps
+        for f, scale in enumerate((4.0 * down, down, down)):
+            for strip in range(strips):
+                for t in range(tiles):
+                    leaving[k, t * strips + strip, f] = scale * state[f, t, band(strip), :]
+
+        def post(j, carry):
+            target = lax.rem(me + j, everyone)
+            send(leaving.at[k, target], out_ref.at[me, k], out_send, out_recv,
+                 target // strips, lax.rem(target, strips))
+            return carry
+
+        lax.fori_loop(1, everyone, post, 0)
+        pltpu.make_async_copy(leaving.at[k, me], out_ref.at[me, k], out_recv).start()
+        return carry
+
+    lax.fori_loop(0, kept, one_mode, 0)
+
+    drain(base_all.at[m, pl.ds(0, strips - 1)], z_send)
+    drain(base_all.at[pl.ds(0, chips - 1)], x_send)
+    drain(base_all.at[pl.ds(0, chips)], p_send)
+    drain(whole.at[:, pl.ds(0, strips - 1)], in_send)
+    drain(leaving.at[:, pl.ds(0, everyone - 1)], out_send)
+    drain(out_ref, out_recv)
+
+
+def step_modes(order, base, land, tangents):
+    strips, tiles = lax.axis_size("rows"), lax.axis_size("mode")
+    held, fields, rows, columns = tangents.shape
+    steps = base.shape[0]
+    kept = held // strips
+    everyone = tiles * strips
     tall = SUB * (strips + 2)
+    vmem = pl.BlockSpec(memory_space=pltpu.VMEM)
+    anywhere = pl.BlockSpec(memory_space=pl.ANY)
+    dma = pltpu.SemaphoreType.DMA
     return pl.pallas_call(
-        functools.partial(steps_kernel, strips, steps, tiles),
-        out_shape=jax.ShapeDtypeStruct((tiles, strips, modes, fields, rows, LANES), jnp.float32),
-        grid_spec=pltpu.PrefetchScalarGridSpec(
-            num_scalar_prefetch=1,
-            grid=(modes,),
-            in_specs=[
-                pl.BlockSpec((strips, 1, fields, rows, columns), lambda k, o: (0, k, 0, 0, 0)),
-                pl.BlockSpec(base.shape, lambda k, o: (0,) * 6, pipeline_mode=pl.Buffered(1)),
-                pl.BlockSpec(land.shape, lambda k, o: (0,) * 3, pipeline_mode=pl.Buffered(1)),
-            ],
-            out_specs=pl.BlockSpec(
-                (tiles, strips, 1, fields, rows, LANES), lambda k, o: (0, 0, k, 0, 0, 0)
-            ),
-            scratch_shapes=[
-                pltpu.VMEM((steps, COEFS, tiles, SUB * strips, LANES), jnp.float32),
-                pltpu.VMEM((tiles, SUB * strips, LANES), jnp.float32),
-                pltpu.VMEM((3, tiles, tall, LANES), jnp.float32),
-                pltpu.VMEM((3, tiles, tall, LANES), jnp.float32),
-                pltpu.VMEM((tiles, tall, LANES), jnp.float32),
-                pltpu.VMEM((2, tiles, tall, LANES), jnp.float32),
-            ],
-        ),
-    )(order, tangents, base, land)
+        functools.partial(steps_kernel, strips, tiles, steps, kept),
+        out_shape=jax.ShapeDtypeStruct((everyone, kept, fields, rows, LANES), jnp.float32),
+        in_specs=[pl.BlockSpec(memory_space=pltpu.SMEM), vmem, vmem, anywhere],
+        out_specs=anywhere,
+        scratch_shapes=[
+            pltpu.VMEM((tiles, strips, steps * fields + 1, rows, LANES), jnp.float32),
+            pltpu.VMEM((kept, strips, fields, rows, columns), jnp.float32),
+            pltpu.VMEM((kept, everyone, fields, rows, LANES), jnp.float32),
+            pltpu.VMEM((steps, COEFS, tiles, SUB * strips, LANES), jnp.float32),
+            pltpu.VMEM((tiles, SUB * strips, LANES), jnp.float32),
+            pltpu.VMEM((3, tiles, tall, LANES), jnp.float32),
+            pltpu.VMEM((3, tiles, tall, LANES), jnp.float32),
+            pltpu.VMEM((tiles, tall, LANES), jnp.float32),
+            pltpu.VMEM((2, tiles, tall, LANES), jnp.float32),
+            dma, dma((strips,)), dma, dma((tiles,)), dma, dma,
+            dma, dma((kept,)), dma, dma,
+        ],
+        compiler_params=pltpu.CompilerParams(collective_id=0, has_side_effects=True),
+    )(order, base, land, tangents)
 
 
 def mix_kernel(coef_ref, cells_ref, out_ref):
@@ -316,18 +402,8 @@
 
 
 def on_device_whole(tangents, checkpoints, owner_order, land_mask, coefficients):
-    strips = lax.axis_size("rows")
-    tiles = lax.axis_size("mode")
-    held, fields, rows, columns = tangents.shape
-    steps = checkpoints.shape[0]
-    base = lax.all_gather(checkpoints, ("mode", "rows"))
-    base = base.reshape(tiles, strips, steps, fields, rows, LANES)
-    land = lax.all_gather(land_mask, "rows")
-    whole = lax.all_to_all(tangents, "rows", split_axis=0, concat_axis=0, tiled=True)
-    whole = whole.reshape(strips, held // strips, fields, rows, columns)
-    done = step_modes(owner_order, whole, base, land)
-    done = done.reshape(tiles * strips, held // strips * fields * rows, LANES)
-    placed = lax.all_to_all(done, ("mode", "rows"), split_axis=0, concat_axis=0, tiled=True)
+    fields, rows = tangents.shape[1:3]
+    placed = step_modes(owner_order, checkpoints, land_mask, tangents)
     mixed = mix(coefficients, placed.reshape(-1, LANES))
     return mixed.reshape(coefficients.shape[0], fields, rows, LANES)
 
@@ -336,7 +412,8 @@
     strips = lax.axis_size("rows")
     held, _, rows, columns = tangents.shape
     fits = (
-        held % strips == 0 and rows == SUB and checkpoints.shape[-1] == LANES and strips <= 8
+        held % strips == 0 and strips > 1 and lax.axis_size("mode") % 2 == 0
+        and lax.axis_size("mode") > 2 and rows == SUB and checkpoints.shape[-1] == LANES and strips <= 8
         and coefficients.shape[0] % LANES == 0
     )
     chosen = on_device_whole if fits else on_device_general

time: 165 us -> 90.5 us (0.55)
  blocking collectives: 88 us -> 0 us
  Pallas kernels: 32.2 us -> 90.3 us
  waiting for transfers between devices: 23.8 us -> 0 us
  between operations: 13.4 us -> 0.01 us
  starting transfers between devices: 6.36 us -> 0 us
    pallas_call x1, Pallas kernels: 28.1 us -> 86.1 us  [step_modes(): pl.pallas_call(functools.partial(steps_kernel, strips, tiles, steps, kept...]
    all_gather x1 -> x0, blocking collectives: 47.8 us -> none  [on_device_whole(): land = lax.all_gather(land_mask, 'rows')]
    all_to_all x1 -> x0, blocking collectives: 40.2 us -> none  [on_device_whole(): lax.all_to_all(done, ('mode', 'rows'), split_axis=0, concat_axis=0, tiled...]
    all_gather x1 -> x0, waiting for transfers between devices: 23 us -> none  [on_device_whole(): base = lax.all_gather(checkpoints, ('mode', 'rows'))]
    all_to_all x1 -> x0, starting transfers between devices: 6.36 us -> none  [on_device_whole(): lax.all_to_all(tangents, 'rows', split_axis=0, concat_axis=0, tiled=True)]
  transfers between devices with their start and end apart: 2 -> 0, of which waited for: 1 -> 0; matrix products, arithmetic and copies ran while one was open for 0% -> 0% of each run, Pallas kernels for 0% -> 0%
where the time goes in v2:
time: 90.5 us; the launch traced here: 90.3 us
  Pallas kernels  90.3 us (100%)
    pallas_call x1, Pallas kernels, step_modes(): pl.pallas_call(functools.partial(steps_kernel, strips, tiles, steps, kept...  86.1 us
    pallas_call x1, Pallas kernels, mix(): pl.pallas_call(mix_kernel, out_shape=jax.ShapeDtypeStruct(cells.shape, jn...  4.17 us

profile of v2, /device:TPU:0, one launch (start us, length us, event | category | flops | bytes accessed | tf_op | source)
XLA Modules:
  0.0 90.3 jit_solution(9827487297452416520)
XLA Ops:
  0.0 86.1 %shard_map.55 = f32[32,4,3,8,128]{4,3,2,1,0:T(8,128)} custom-call(s32[8]{0:T(128)} %order.1, f32[8,3,8,128]{3,2,1,0:T(8,128)} %base_ref.1, s32[8,1024]{1,0:T(8,128)} %land_ref.1, f32[16,3,8,1024]{3,2,1,0:T(8,128)} %tan_ref.1), custom_call_target="tpu_custom_call" | custom-call | tf_op jit(solution)/shard_map/pallas_call | solution.py:359
  86.1 4.2 %shard_map.56 = f32[3072,128]{1,0:T(8,128)} custom-call(f32[128,128]{1,0:T(8,128)} %coef_ref.1, f32[3072,128]{1,0:T(8,128)} %bitcast.2), custom_call_target="tpu_custom_call" | custom-call | tf_op jit(solution)/shard_map/pallas_call | solution.py:396

commit v3 on v2

--- a/solution.py
+++ b/solution.py
@@ -238,7 +238,7 @@
 def steps_kernel(strips, tiles, steps, kept, order, base_ref, land_ref, tan_ref, out_ref,
                  base_all, whole, leaving, coef, wet, state, middle, flux, flow_pad,
                  z_send, z_recv, x_send, x_recv, p_send, p_recv,
-                 in_send, in_recv, out_send, out_recv):
+                 in_send, in_recv, out_send, out_recv, known):
     m = lax.axis_index("mode")
     r = lax.axis_index("rows")
     everyone = tiles * strips
@@ -264,40 +264,61 @@
 
     barrier = pltpu.get_barrier_semaphore()
 
-    def greet(j, carry):
-        target = lax.rem(me + j, everyone)
+    def signal(sem, mode, row):
         pl.semaphore_signal(
-            barrier, inc=1, device_id=(target // strips, lax.rem(target, strips)),
-            device_id_type=pl.DeviceIdType.MESH,
-        )
-        return carry
-
-    lax.fori_loop(1, everyone, greet, 0)
+            sem, inc=1, device_id=(mode, row), device_id_type=pl.DeviceIdType.MESH
+        )
+
+    for j in range(1, strips):
+        signal(barrier, m, lax.rem(r + j, strips))
+    for j in range(1, tiles):
+        signal(barrier, lax.rem(m + j, tiles), r)
 
     own = base_all.at[m, r]
     own[pl.ds(0, mask_at)] = base_ref[...].reshape(mask_at, SUB, LANES)
     own[mask_at] = land_ref[:, pl.ds(pl.multiple_of(m * LANES, LANES), LANES)].astype(jnp.float32)
 
-    pl.semaphore_wait(barrier, everyone - 1)
-
+    pl.semaphore_wait(barrier, strips + tiles - 2)
+
+    def send_in(k, j):
+        q = lax.rem(r + j, strips)
+        send(tan_ref.at[q * kept + k], whole.at[k, r], in_send, in_recv.at[k], m, q)
+
+    def relay(q):
+        strip = base_all.at[m, q]
+
+        @pl.when(jnp.logical_and(q <= r, r < strips - 1))
+        def _():
+            send(strip, strip, z_send.at[0, q], z_recv.at[q], m, r + 1)
+
+        @pl.when(jnp.logical_and(q >= r, r > 0))
+        def _():
+            send(strip, strip, z_send.at[1, q], z_recv.at[q], m, r - 1)
+
+        for j in range(1, chips):
+            send(strip, strip, x_send, x_recv.at[m], other_chip(j), r)
+
+    relay(r)
     for j in range(1, strips):
-        q = lax.rem(r + j, strips)
-        send(own, own, z_send, z_recv.at[r], m, q)
-    for j in range(1, chips):
-        send(own, own, x_send, x_recv.at[m], other_chip(j), r)
+        send_in(0, j)
+
+        @pl.when(r >= j)
+        def _():
+            drain(base_all.at[m, r - j], z_recv.at[r - j])
+            relay(r - j)
+
+        @pl.when(r + j < strips)
+        def _():
+            drain(base_all.at[m, r + j], z_recv.at[r + j])
+            relay(r + j)
 
     for k in range(kept):
-        for j in range(1, strips):
-            q = lax.rem(r + j, strips)
-            send(tan_ref.at[q * kept + k], whole.at[k, r], in_send, in_recv.at[k], m, q)
+        if k > 0:
+            for j in range(1, strips):
+                send_in(k, j)
         pltpu.make_async_copy(tan_ref.at[r * kept + k], whole.at[k, r], in_recv.at[k]).start()
-
-    for j in range(1, strips):
-        q = lax.rem(r + j, strips)
-        strip = base_all.at[m, q]
-        drain(strip, z_recv.at[q])
-        for i in range(1, chips):
-            send(strip, strip, x_send, x_recv.at[m], other_chip(i), r)
+    for j in range(1, tiles):
+        signal(known, lax.rem(m + j, tiles), r)
     send(base_all.at[m], base_all.at[m], p_send, p_recv, partner, r)
     for ref in (state, middle, flux):
         zero_pads(ref, strips)
@@ -336,9 +357,19 @@
         pltpu.make_async_copy(leaving.at[k, me], out_ref.at[me, k], out_recv).start()
         return carry
 
+    pl.semaphore_wait(known, tiles - 1)
     lax.fori_loop(0, kept, one_mode, 0)
 
-    drain(base_all.at[m, pl.ds(0, strips - 1)], z_send)
+    for q in range(strips):
+
+        @pl.when(jnp.logical_and(q <= r, r < strips - 1))
+        def _():
+            drain(base_all.at[m, q], z_send.at[0, q])
+
+        @pl.when(jnp.logical_and(q >= r, r > 0))
+        def _():
+            drain(base_all.at[m, q], z_send.at[1, q])
+
     drain(base_all.at[pl.ds(0, chips - 1)], x_send)
     drain(base_all.at[pl.ds(0, chips)], p_send)
     drain(whole.at[:, pl.ds(0, strips - 1)], in_send)
@@ -371,40 +402,64 @@
             pltpu.VMEM((3, tiles, tall, LANES), jnp.float32),
             pltpu.VMEM((tiles, tall, LANES), jnp.float32),
             pltpu.VMEM((2, tiles, tall, LANES), jnp.float32),
-            dma, dma((strips,)), dma, dma((tiles,)), dma, dma,
-            dma, dma((kept,)), dma, dma,
+            dma((2, strips)), dma((strips,)), dma, dma((tiles,)), dma, dma,
+            dma, dma((kept,)), dma, dma, pltpu.SemaphoreType.REGULAR,
         ],
         compiler_params=pltpu.CompilerParams(collective_id=0, has_side_effects=True),
     )(order, base, land, tangents)
 
 
-def mix_kernel(coef_ref, cells_ref, out_ref):
-    modes = coef_ref.shape[0]
-    row = lax.broadcasted_iota(jnp.int32, (modes, modes), 0)
-    col = lax.broadcasted_iota(jnp.int32, (modes, modes), 1)
-    mixing = jnp.where(row <= col, coef_ref[...], 0.0) + jnp.where(row == col, 1.0, 0.0)
-    turned = mixing.T
-    per = cells_ref.shape[0] // modes
-    for spot in range(per):
-        cells = cells_ref[pl.ds(spot, modes, stride=per), :]
-        out_ref[pl.ds(spot, modes, stride=per), :] = jnp.dot(
-            turned, cells, precision=lax.Precision.HIGHEST, preferred_element_type=jnp.float32
-        )
+def halves(values):
+    high = values.astype(jnp.bfloat16)
+    return high, (values - high.astype(jnp.float32)).astype(jnp.bfloat16)
+
+
+def mix_kernel(coef_ref, cells_ref, out_ref, turned):
+    modes, rows, _ = cells_ref.shape
+
+    @pl.when(pl.program_id(0) == 0)
+    def _():
+        row = lax.broadcasted_iota(jnp.int32, (modes, modes), 0)
+        col = lax.broadcasted_iota(jnp.int32, (modes, modes), 1)
+        mixing = jnp.where(row <= col, coef_ref[...], 0.0) + jnp.where(row == col, 1.0, 0.0)
+        high, low = halves(mixing.T)
+        turned[...] = jnp.concatenate(
+            [jnp.concatenate([high, high], 1), jnp.concatenate([low, low], 1)], 0
+        )
+
+    cells = cells_ref.reshape(modes * rows, LANES)
+    out = out_ref.reshape(modes * rows, LANES)
+    for spot in range(0, rows, 2):
+        high, low = halves(
+            jnp.concatenate([cells[pl.ds(spot + i, modes, stride=rows), :] for i in (0, 1)], 1)
+        )
+        mixed = jnp.dot(
+            turned[...], jnp.concatenate([high, low], 0), preferred_element_type=jnp.float32
+        )
+        mixed = mixed[:modes] + mixed[modes:]
+        for i in (0, 1):
+            out[pl.ds(spot + i, modes, stride=rows), :] = mixed[:, LANES * i:LANES * (i + 1)]
 
 
 def mix(coefficients, cells):
+    modes, spots, _ = cells.shape
     return pl.pallas_call(
         mix_kernel,
         out_shape=jax.ShapeDtypeStruct(cells.shape, jnp.float32),
-        in_specs=[pl.BlockSpec(memory_space=pltpu.VMEM)] * 2,
-        out_specs=pl.BlockSpec(memory_space=pltpu.VMEM),
+        grid=(spots // SUB,),
+        in_specs=[
+            pl.BlockSpec((modes, modes), lambda i: (0, 0), pipeline_mode=pl.Buffered(1)),
+            pl.BlockSpec((modes, SUB, LANES), lambda i: (0, i, 0)),
+        ],
+        out_specs=pl.BlockSpec((modes, SUB, LANES), lambda i: (0, i, 0)),
+        scratch_shapes=[pltpu.VMEM((2 * modes, 2 * modes), jnp.bfloat16)],
     )(coefficients, cells)
 
 
 def on_device_whole(tangents, checkpoints, owner_order, land_mask, coefficients):
     fields, rows = tangents.shape[1:3]
     placed = step_modes(owner_order, checkpoints, land_mask, tangents)
-    mixed = mix(coefficients, placed.reshape(-1, LANES))
+    mixed = mix(coefficients, placed.reshape(coefficients.shape[0], fields * rows, LANES))
     return mixed.reshape(coefficients.shape[0], fields, rows, LANES)
 
 

time: 90.5 us -> 85.7 us (0.947)
  Pallas kernels: 90.3 us -> 85.5 us
    pallas_call x1, Pallas kernels: 86.1 us -> 81.6 us  [step_modes(): pl.pallas_call(functools.partial(steps_kernel, strips, tiles, steps, kept...]
where the time goes in v3:
time: 85.7 us; the launch traced here: 85.5 us
  Pallas kernels  85.5 us (100%)
    pallas_call x1, Pallas kernels, step_modes(): pl.pallas_call(functools.partial(steps_kernel, strips, tiles, steps, kept...  81.6 us
    pallas_call x1, Pallas kernels, mix(): pl.pallas_call(mix_kernel, out_shape=jax.ShapeDtypeStruct(cells.shape, jn...  3.9 us

profile of v3, /device:TPU:0, one launch (start us, length us, event | category | flops | bytes accessed | tf_op | source)
XLA Modules:
  0.0 85.5 jit_solution(2242061313810579140)
XLA Ops:
  0.0 81.6 %shard_map.55 = f32[32,4,3,8,128]{4,3,2,1,0:T(8,128)} custom-call(s32[8]{0:T(128)} %order.1, f32[8,3,8,128]{3,2,1,0:T(8,128)} %base_ref.1, s32[8,1024]{1,0:T(8,128)} %land_ref.1, f32[16,3,8,1024]{3,2,1,0:T(8,128)} %tan_ref.1), custom_call_target="tpu_custom_call" | custom-call | tf_op jit(solution)/shard_map/pallas_call | solution.py:390
  81.6 3.9 %shard_map.56 = f32[128,24,128]{2,1,0:T(8,128)} custom-call(f32[128,128]{1,0:T(8,128)} %coef_ref.1, f32[128,24,128]{2,1,0:T(8,128)} %bitcast.2), custom_call_target="tpu_custom_call" | custom-call | tf_op jit(solution)/shard_map/pallas_call | solution.py:446

commit v4 on v3

--- a/solution.py
+++ b/solution.py
@@ -235,10 +235,10 @@
     lax.fori_loop(0, steps, one, 0)
 
 
-def steps_kernel(strips, tiles, steps, kept, order, base_ref, land_ref, tan_ref, out_ref,
+def steps_kernel(strips, tiles, steps, kept, order_ref, base_ref, land_ref, tan_ref, out_ref,
                  base_all, whole, leaving, coef, wet, state, middle, flux, flow_pad,
                  z_send, z_recv, x_send, x_recv, p_send, p_recv,
-                 in_send, in_recv, out_send, out_recv, known):
+                 in_send, in_recv, out_send, out_recv, known, land, order, fetch):
     m = lax.axis_index("mode")
     r = lax.axis_index("rows")
     everyone = tiles * strips
@@ -275,8 +275,17 @@
         signal(barrier, lax.rem(m + j, tiles), r)
 
     own = base_all.at[m, r]
-    own[pl.ds(0, mask_at)] = base_ref[...].reshape(mask_at, SUB, LANES)
-    own[mask_at] = land_ref[:, pl.ds(pl.multiple_of(m * LANES, LANES), LANES)].astype(jnp.float32)
+    tile_of_land = land_ref.at[:, pl.ds(pl.multiple_of(m * LANES, LANES), LANES)]
+    fetch_base = pltpu.make_async_copy(base_ref, own.at[pl.ds(0, mask_at)], fetch.at[0])
+    fetch_land = pltpu.make_async_copy(tile_of_land, land, fetch.at[1])
+    fetch_order = pltpu.make_async_copy(order_ref, order, fetch.at[2])
+    fetch_base.start()
+    fetch_land.start()
+    fetch_order.start()
+    fetch_land.wait()
+    own[mask_at] = land[...].astype(jnp.float32)
+    fetch_base.wait()
+    fetch_order.wait()
 
     pl.semaphore_wait(barrier, strips + tiles - 2)
 
@@ -347,13 +356,18 @@
                 for t in range(tiles):
                     leaving[k, t * strips + strip, f] = scale * state[f, t, band(strip), :]
 
-        def post(j, carry):
-            target = lax.rem(me + j, everyone)
-            send(leaving.at[k, target], out_ref.at[me, k], out_send, out_recv,
-                 target // strips, lax.rem(target, strips))
-            return carry
-
-        lax.fori_loop(1, everyone, post, 0)
+        def post(row):
+            def to(j, carry):
+                mode = lax.rem(m + j, tiles)
+                send(leaving.at[k, mode * strips + row], out_ref.at[me, k], out_send, out_recv,
+                     mode, row)
+                return carry
+
+            return to
+
+        for j in range(strips):
+            row = lax.rem(r + strips // 2 + j, strips)
+            lax.fori_loop(1 if j == strips - strips // 2 else 0, tiles, post(row), 0)
         pltpu.make_async_copy(leaving.at[k, me], out_ref.at[me, k], out_recv).start()
         return carry
 
@@ -384,14 +398,14 @@
     kept = held // strips
     everyone = tiles * strips
     tall = SUB * (strips + 2)
-    vmem = pl.BlockSpec(memory_space=pltpu.VMEM)
-    anywhere = pl.BlockSpec(memory_space=pl.ANY)
+    hbm = pl.BlockSpec(memory_space=pltpu.HBM)
+    operands = (order, base.reshape(steps * fields, rows, LANES), land, tangents)
     dma = pltpu.SemaphoreType.DMA
     return pl.pallas_call(
         functools.partial(steps_kernel, strips, tiles, steps, kept),
         out_shape=jax.ShapeDtypeStruct((everyone, kept, fields, rows, LANES), jnp.float32),
-        in_specs=[pl.BlockSpec(memory_space=pltpu.SMEM), vmem, vmem, anywhere],
-        out_specs=anywhere,
+        in_specs=[hbm] * 4,
+        out_specs=pl.BlockSpec(memory_space=pl.ANY),
         scratch_shapes=[
             pltpu.VMEM((tiles, strips, steps * fields + 1, rows, LANES), jnp.float32),
             pltpu.VMEM((kept, strips, fields, rows, columns), jnp.float32),
@@ -404,9 +418,12 @@
             pltpu.VMEM((2, tiles, tall, LANES), jnp.float32),
             dma((2, strips)), dma((strips,)), dma, dma((tiles,)), dma, dma,
             dma, dma((kept,)), dma, dma, pltpu.SemaphoreType.REGULAR,
+            pltpu.VMEM((rows, LANES), jnp.int32), pltpu.SMEM((steps,), jnp.int32), dma((3,)),
         ],
-        compiler_params=pltpu.CompilerParams(collective_id=0, has_side_effects=True),
-    )(order, base, land, tangents)
+        compiler_params=pltpu.CompilerParams(
+            collective_id=0, has_side_effects=True, vmem_limit_bytes=24 << 20
+        ),
+    )(*(pltpu.with_memory_space_constraint(held_in_hbm, pltpu.HBM) for held_in_hbm in operands))
 
 
 def halves(values):
@@ -415,7 +432,9 @@
 
 
 def mix_kernel(coef_ref, cells_ref, out_ref, turned):
-    modes, rows, _ = cells_ref.shape
+    modes, rows, _ = out_ref.shape
+    spots = cells_ref.shape[1]
+    first = rows * pl.program_id(0)
 
     @pl.when(pl.program_id(0) == 0)
     def _():
@@ -427,11 +446,11 @@
             [jnp.concatenate([high, high], 1), jnp.concatenate([low, low], 1)], 0
         )
 
-    cells = cells_ref.reshape(modes * rows, LANES)
+    cells = cells_ref.reshape(modes * spots, LANES)
     out = out_ref.reshape(modes * rows, LANES)
     for spot in range(0, rows, 2):
         high, low = halves(
-            jnp.concatenate([cells[pl.ds(spot + i, modes, stride=rows), :] for i in (0, 1)], 1)
+            jnp.concatenate([cells[pl.ds(first + spot + i, modes, stride=spots), :] for i in (0, 1)], 1)
         )
         mixed = jnp.dot(
             turned[...], jnp.concatenate([high, low], 0), preferred_element_type=jnp.float32
@@ -449,10 +468,11 @@
         grid=(spots // SUB,),
         in_specs=[
             pl.BlockSpec((modes, modes), lambda i: (0, 0), pipeline_mode=pl.Buffered(1)),
-            pl.BlockSpec((modes, SUB, LANES), lambda i: (0, i, 0)),
+            pl.BlockSpec(memory_space=pltpu.VMEM),
         ],
         out_specs=pl.BlockSpec((modes, SUB, LANES), lambda i: (0, i, 0)),
         scratch_shapes=[pltpu.VMEM((2 * modes, 2 * modes), jnp.bfloat16)],
+        compiler_params=pltpu.CompilerParams(vmem_limit_bytes=8 << 20),
     )(coefficients, cells)
 
 

time: 85.7 us -> 81.6 us (0.952)
  Pallas kernels: 85.5 us -> 81.4 us
    pallas_call x1, Pallas kernels: 81.6 us -> 79 us  [step_modes(): pl.pallas_call(functools.partial(steps_kernel, strips, tiles, steps, kept...]
    pallas_call x1, Pallas kernels: 3.9 us -> 2.42 us  [mix(): pl.pallas_call(mix_kernel, out_shape=jax.ShapeDtypeStruct(cells.shape, jn...]
where the time goes in v4:
time: 81.6 us; the launch traced here: 81.5 us
  Pallas kernels  81.4 us (100%)
    pallas_call x1, Pallas kernels, step_modes(): pl.pallas_call(functools.partial(steps_kernel, strips, tiles, steps, kept...  79 us
    pallas_call x1, Pallas kernels, mix(): pl.pallas_call(mix_kernel, out_shape=jax.ShapeDtypeStruct(cells.shape, jn...  2.42 us

profile of v4, /device:TPU:0, one launch (start us, length us, event | category | flops | bytes accessed | tf_op | source)
XLA Modules:
  0.0 81.5 jit_solution(3741951967284729674)
XLA Ops:
  0.0 0.0 copy-start
  0.0 79.0 %shard_map.55 = f32[32,4,3,8,128]{4,3,2,1,0:T(8,128)S(1)} custom-call(s32[8]{0:T(128)} %order_ref.1, f32[24,8,128]{2,1,0:T(8,128)} %bitcast.4, s32[8,1024]{1,0:T(8,128)} %land_ref.1, f32[16,3,8,1024]{3,2,1,0:T(8,128)} %tan_ref.1), custom_call_target="tpu_custom_call" | custom-call | tf_op jit(solution)/shard_map/pallas_call | solution.py:404
  79.0 0.0 copy-done
  79.0 2.4 %shard_map.56 = f32[128,24,128]{2,1,0:T(8,128)} custom-call(f32[128,128]{1,0:T(8,128)S(1)} %copy-done, f32[128,24,128]{2,1,0:T(8,128)S(1)} %bitcast.3), custom_call_target="tpu_custom_call" | custom-call | tf_op jit(solution)/shard_map/pallas_call | solution.py:465
Async XLA Ops:
  0.0 79.0 %copy-start = (f32[128,128]{1,0:T(8,128)S(1)}, f32[128,128]{1,0:T(8,128)}, u32[]{:S(2)}) copy-start(f32[128,128]{1,0:T(8,128)} %coef_ref.1) | copy-start | bytes 196612

commit v5 on v4

--- a/solution.py
+++ b/solution.py
@@ -431,33 +431,36 @@
     return high, (values - high.astype(jnp.float32)).astype(jnp.bfloat16)
 
 
-def mix_kernel(coef_ref, cells_ref, out_ref, turned):
-    modes, rows, _ = out_ref.shape
-    spots = cells_ref.shape[1]
-    first = rows * pl.program_id(0)
-
-    @pl.when(pl.program_id(0) == 0)
-    def _():
-        row = lax.broadcasted_iota(jnp.int32, (modes, modes), 0)
-        col = lax.broadcasted_iota(jnp.int32, (modes, modes), 1)
-        mixing = jnp.where(row <= col, coef_ref[...], 0.0) + jnp.where(row == col, 1.0, 0.0)
-        high, low = halves(mixing.T)
-        turned[...] = jnp.concatenate(
-            [jnp.concatenate([high, high], 1), jnp.concatenate([low, low], 1)], 0
-        )
-
+def mix_kernel(coef_ref, cells_ref, out_ref, staged, sems):
+    modes, spots, _ = cells_ref.shape
+    row = lax.broadcasted_iota(jnp.int32, (modes, modes), 0)
+    col = lax.broadcasted_iota(jnp.int32, (modes, modes), 1)
+    mixing = jnp.where(row <= col, coef_ref[...], 0.0) + jnp.where(row == col, 1.0, 0.0)
+    high, low = halves(mixing.T)
+    turned = jnp.concatenate(
+        [jnp.concatenate([high, high], 1), jnp.concatenate([low, low], 1)], 0
+    )
     cells = cells_ref.reshape(modes * spots, LANES)
-    out = out_ref.reshape(modes * rows, LANES)
-    for spot in range(0, rows, 2):
-        high, low = halves(
-            jnp.concatenate([cells[pl.ds(first + spot + i, modes, stride=spots), :] for i in (0, 1)], 1)
-        )
-        mixed = jnp.dot(
-            turned[...], jnp.concatenate([high, low], 0), preferred_element_type=jnp.float32
-        )
-        mixed = mixed[:modes] + mixed[modes:]
-        for i in (0, 1):
-            out[pl.ds(spot + i, modes, stride=rows), :] = mixed[:, LANES * i:LANES * (i + 1)]
+    copies = []
+    for group in range(spots // SUB):
+        out = staged.at[group].reshape(modes * SUB, LANES)
+        for spot in range(0, SUB, 2):
+            first = SUB * group + spot
+            high, low = halves(jnp.concatenate(
+                [cells[pl.ds(first + i, modes, stride=spots), :] for i in (0, 1)], 1
+            ))
+            mixed = jnp.dot(
+                turned, jnp.concatenate([high, low], 0), preferred_element_type=jnp.float32
+            )
+            mixed = mixed[:modes] + mixed[modes:]
+            for i in (0, 1):
+                out[pl.ds(spot + i, modes, stride=SUB), :] = mixed[:, LANES * i:LANES * (i + 1)]
+        copies.append(pltpu.make_async_copy(
+            staged.at[group], out_ref.at[:, pl.ds(SUB * group, SUB)], sems.at[group]
+        ))
+        copies[-1].start()
+    for copy in copies:
+        copy.wait()
 
 
 def mix(coefficients, cells):
@@ -465,13 +468,12 @@
     return pl.pallas_call(
         mix_kernel,
         out_shape=jax.ShapeDtypeStruct(cells.shape, jnp.float32),
-        grid=(spots // SUB,),
-        in_specs=[
-            pl.BlockSpec((modes, modes), lambda i: (0, 0), pipeline_mode=pl.Buffered(1)),
-            pl.BlockSpec(memory_space=pltpu.VMEM),
+        in_specs=[pl.BlockSpec(memory_space=pltpu.VMEM)] * 2,
+        out_specs=pl.BlockSpec(memory_space=pltpu.HBM),
+        scratch_shapes=[
+            pltpu.VMEM((spots // SUB, modes, SUB, LANES), jnp.float32),
+            pltpu.SemaphoreType.DMA((spots // SUB,)),
         ],
-        out_specs=pl.BlockSpec((modes, SUB, LANES), lambda i: (0, i, 0)),
-        scratch_shapes=[pltpu.VMEM((2 * modes, 2 * modes), jnp.bfloat16)],
         compiler_params=pltpu.CompilerParams(vmem_limit_bytes=8 << 20),
     )(coefficients, cells)
 

time: 81.6 us -> 80.8 us (level)
  no operation moved by 1% of the time
where the time goes in v5:
time: 80.8 us; the launch traced here: 80.6 us
  Pallas kernels  80.6 us (100%)
    pallas_call x1, Pallas kernels, step_modes(): pl.pallas_call(functools.partial(steps_kernel, strips, tiles, steps, kept...  79 us

profile of v5, /device:TPU:0, one launch (start us, length us, event | category | flops | bytes accessed | tf_op | source)
XLA Modules:
  0.0 80.6 jit_solution(11525861423642117754)
XLA Ops:
  0.0 0.0 copy-start
  0.0 79.0 %shard_map.55 = f32[32,4,3,8,128]{4,3,2,1,0:T(8,128)S(1)} custom-call(s32[8]{0:T(128)} %order_ref.1, f32[24,8,128]{2,1,0:T(8,128)} %bitcast.4, s32[8,1024]{1,0:T(8,128)} %land_ref.1, f32[16,3,8,1024]{3,2,1,0:T(8,128)} %tan_ref.1), custom_call_target="tpu_custom_call" | custom-call | tf_op jit(solution)/shard_map/pallas_call | solution.py:404
  79.0 0.0 copy-done
  79.0 1.6 %shard_map.56 = f32[128,24,128]{2,1,0:T(8,128)} custom-call(f32[128,128]{1,0:T(8,128)S(1)} %copy-done, f32[128,24,128]{2,1,0:T(8,128)S(1)} %bitcast.3), custom_call_target="tpu_custom_call" | custom-call | tf_op jit(solution)/shard_map/pallas_call | solution.py:468
Async XLA Ops:
  0.0 79.0 %copy-start = (f32[128,128]{1,0:T(8,128)S(1)}, f32[128,128]{1,0:T(8,128)}, u32[]{:S(2)}) copy-start(f32[128,128]{1,0:T(8,128)} %coef_ref.1) | copy-start | bytes 196612
